TPU v7x, 32 devices: a whole 2x2x4 slice. The times are simulated.
32 devices in a mesh: groups: 2 (over x), depth: 16 (over z, y, core).
Axes of the slice: x: 2, y: 2, z: 4, core: 2. Of those that a mesh axis runs over, the one named last changes fastest.
Arguments:
- voxels: bfloat16 [256, 32, 16384], P(('groups', 'depth')), parts along dimension 0, may hold values from -6 to 6
- offsets: int32 [256], P('groups'), parts along dimension 0, may hold values from 0 to 127
- w_first: bfloat16 [64, 32], replicated, may hold values from -1 to 1
- decoder_second_weight: bfloat16 [33, 64], replicated, may hold values from -0.75 to 0.75
- cotangent: float32 [32, 32768], P(None, ('groups', 'depth')), parts along dimension 1, may hold values from -6 to 6
Outputs:
- image: float32 [32, 32768], P(None, ('groups', 'depth')), parts along dimension 1
- grad_voxels: bfloat16 [256, 32, 16384], P(('groups', 'depth')), parts along dimension 0
- grad_first: float32 [128, 32], P('groups'), parts along dimension 0
- grad_second: float32 [66, 64], P('groups'), parts along dimension 0
There are 2 independent parts, one for each index of `groups`. A program takes and returns all parts, laid end to end along the dimension named above; an argument that names none is the same for every part. Nothing has to cross between parts.
Inputs may be any that keep to these rules, and one draw needn't show every extreme that they name: offsets[p] counts tiles of 128 rays.
All inputs are finite; a program needn't handle non-finite values.
Results may differ from a plain program's by a relative error of at most 0.0085.
Values may be sent and summed in bfloat16 or wider, within the bound.
A program may use at most 192 MiB of HBM per device.

v0:
```python
import jax
import jax.numpy as jnp
from jax import lax
from jax.sharding import PartitionSpec as P

TILE = 128


def carried_in(x, axis, combine, identity):
    length, position = (lax.axis_size(axis), lax.axis_index(axis))
    everything = jax.tree.map(lambda part: lax.all_gather(part, axis), x)
    start = jax.tree.map(
        lambda part, zero: jnp.broadcast_to(jnp.asarray(zero, part.dtype), part.shape), x, identity
    )

    def step(k, before):
        reached = k < position
        new = combine(before, jax.tree.map(lambda part: part[k], everything))
        return jax.tree.map(lambda a, b: jnp.where(reached, a, b), new, before)

    return lax.fori_loop(0, length, step, start)


def decode_plane(plane, w_first, decoder_second_weight):
    preact = jnp.dot(w_first, plane, preferred_element_type=jnp.float32)
    hidden = jax.nn.silu(preact).astype(jnp.bfloat16)
    output_raw = jnp.dot(decoder_second_weight, hidden, preferred_element_type=jnp.float32)
    return (preact, hidden, output_raw)


def make_slab(output_raw, dscale):
    channels = output_raw.shape[0] - 1
    emitted_light = jax.nn.sigmoid(output_raw[:channels])
    density = jax.nn.softplus(output_raw[channels]) * dscale
    return jnp.concatenate([emitted_light, density[None]], 0).astype(jnp.bfloat16)


def move_rays(values, start):
    doubled = jnp.concatenate([values, values], values.ndim - 1)
    return lax.dynamic_slice_in_dim(doubled, start, values.shape[-1], values.ndim - 1)


def blended_image(slabs, upstream_gradient):
    channels = slabs.shape[1] - 1
    emitted_light = slabs[:, :channels].astype(jnp.float32)
    density = slabs[:, channels].astype(jnp.float32)
    passing = jnp.exp(-density)
    through = jnp.cumprod(passing, axis=0)
    before = jnp.concatenate([jnp.ones_like(through[:1]), through[:-1]], 0)
    sample_weight_rows = before * (1.0 - passing)
    pixel_colour = jnp.einsum("vi,vsi->si", sample_weight_rows, emitted_light)
    objective_value = jnp.einsum("vz,dvz->dz", upstream_gradient, emitted_light)
    running = jnp.cumsum(sample_weight_rows * objective_value, axis=0)
    return (
        passing,
        before,
        sample_weight_rows,
        objective_value,
        running,
        through[-1],
        pixel_colour,
    )


def slab_gradient(
    passing,
    before,
    sample_weight_rows,
    objective_value,
    running,
    upstream_gradient,
    enter,
    prior,
    ray_total,
):
    grad_rad = (enter * sample_weight_rows)[:, None, :] * upstream_gradient[None]
    grad_dens = enter * before * passing * objective_value - (ray_total - (prior + enter * running))
    return jnp.concatenate([grad_rad, grad_dens[:, None, :]], 1).astype(jnp.bfloat16)


def plane_backward(carry, inputs, w_first, decoder_second_weight, dscale):
    plane, grad_sheared, shift_tiles = inputs
    rays_count = plane.shape[1]
    preact, hidden, output_raw = decode_plane(plane, w_first, decoder_second_weight)
    grad_slab = move_rays(grad_sheared, rays_count - TILE * shift_tiles).astype(jnp.float32)
    channels = output_raw.shape[0] - 1
    sig_rad = jax.nn.sigmoid(output_raw[:channels])
    grad_rad = grad_slab[:channels] * sig_rad * (1.0 - sig_rad)
    grad_dens = grad_slab[channels] * dscale * jax.nn.sigmoid(output_raw[channels])
    grad_raw = jnp.concatenate([grad_rad, grad_dens[None]], 0).astype(jnp.bfloat16)
    grad_hidden = jnp.dot(decoder_second_weight.T, grad_raw, preferred_element_type=jnp.float32)
    sig_pre = jax.nn.sigmoid(preact)
    grad_pre = (grad_hidden * sig_pre * (1.0 + preact * (1.0 - sig_pre))).astype(jnp.bfloat16)
    grad_plane = jnp.dot(w_first.T, grad_pre, preferred_element_type=jnp.float32).astype(
        jnp.bfloat16
    )
    contract = (((1,), (1,)), ((), ()))
    acc_first = carry[0] + lax.dot_general(
        grad_pre, plane, contract, preferred_element_type=jnp.float32
    )
    acc_second = carry[1] + lax.dot_general(
        grad_raw, hidden, contract, preferred_element_type=jnp.float32
    )
    return ((acc_first, acc_second), grad_plane)


def join_depth(preceding_samples, later):
    return (preceding_samples[0] * later[0], preceding_samples[1] + preceding_samples[0] * later[1])


def shards(voxels, offsets, w_first, decoder_second_weight, cotangent):
    planes_here = voxels.shape[0]
    rays_count = voxels.shape[2]
    dscale = 3.0 / (planes_here * lax.axis_size("depth"))
    my_offsets = lax.dynamic_slice_in_dim(
        offsets, lax.axis_index("depth") * planes_here, planes_here
    )

    def forward_plane(inputs):
        plane, shift_tiles = inputs
        output_raw = decode_plane(plane, w_first, decoder_second_weight)[2]
        return move_rays(make_slab(output_raw, dscale), TILE * shift_tiles)

    slabs = lax.map(forward_plane, (voxels, my_offsets))
    cotan_full = lax.all_gather(cotangent, "depth", axis=1, tiled=True)
    passing, before, sample_weight_rows, objective_value, running, last_pass, pixel_colour = (
        blended_image(slabs, cotan_full)
    )
    identity = (jnp.ones((rays_count,), jnp.float32), jnp.zeros((rays_count,), jnp.float32))
    enter, prior = carried_in((last_pass, running[-1]), "depth", join_depth, identity)
    image = lax.psum_scatter(
        (enter[None, :] * pixel_colour).astype(jnp.bfloat16),
        "depth",
        scatter_dimension=1,
        tiled=True,
    ).astype(jnp.float32)
    ray_total = lax.psum(enter * running[-1], "depth")
    grad_sheared = slab_gradient(
        passing,
        before,
        sample_weight_rows,
        objective_value,
        running,
        cotan_full,
        enter,
        prior,
        ray_total,
    )

    def step_plane(carry, inputs):
        return plane_backward(carry, inputs, w_first, decoder_second_weight, dscale)

    start = (
        jnp.zeros(w_first.shape, jnp.float32),
        jnp.zeros(decoder_second_weight.shape, jnp.float32),
    )
    grads, grad_voxels = lax.scan(step_plane, start, (voxels, grad_sheared, my_offsets))
    grad_first, grad_second = lax.psum((grads[0], grads[1]), "depth")
    return (image, grad_voxels, grad_first, grad_second)


def solution(mesh):
    placed = (
        P(("groups", "depth"), None, None),
        P("groups"),
        P(),
        P(),
        P(None, ("groups", "depth")),
    )
    return jax.shard_map(
        shards,
        mesh=mesh,
        in_specs=placed,
        out_specs=(
            P(None, ("groups", "depth")),
            P(("groups", "depth"), None, None),
            P("groups", None),
            P("groups", None),
        ),
        check_vma=False,
    )
```

profile of v0, /device:TPU:0, one launch (start us, length us, event | category | flops | bytes accessed | tf_op | source)
XLA Modules:
  0.0 509.5 jit_solution(6826601035161955763)
XLA Ops:
  8.7 59.9 %while.43 = (s32[]{:T(128)}, bf16[8,33,16384]{2,1,0:T(8,128)(2,1)}, bf16[8,32,16384]{2,1,0:T(8,128)(2,1)}, bf16[64,32]{0,1:T(8,128)(2,1)}, bf16[33,64]{1,0:T(8,1...) while((s32[]{:T(128)}, bf16[8,33,16384]{2,1,0:T(8,128)(2,1)}, ...), condition=%wide.region_1.2_spmd, body=%wide.region_0.1_spmd.sunk | while | flops 148111360 | bytes 8865971 | solution.py:124
  9.9 3.1 convolution_bitcast_fusion.7
  13.9 2.3 fusion.82
  17.4 3.1 convolution_bitcast_fusion.7
  21.4 2.3 fusion.82
  24.9 3.1 convolution_bitcast_fusion.7
  28.9 2.3 fusion.82
  32.4 3.1 convolution_bitcast_fusion.7
  36.3 2.3 fusion.82
  39.8 3.1 convolution_bitcast_fusion.7
  43.8 2.3 fusion.82
  47.3 3.1 convolution_bitcast_fusion.7
  51.3 2.3 fusion.82
  54.8 3.1 convolution_bitcast_fusion.7
  58.8 2.3 fusion.82
  62.3 3.1 convolution_bitcast_fusion.7
  66.3 2.2 fusion.82
  68.6 12.2 %copy.12 = bf16[8,33,16384]{2,0,1:T(8,128)(2,1)} copy(bf16[8,33,16384]{2,1,0:T(8,128)(2,1)} %get-tuple-element.261) | data formatting | bytes 17301504 | tf_op jit(solution)/shard_map/while | solution.py:124
  83.3 6.6 %multiply_reduce_fusion.1 = f32[16384,8]{0,1:T(8,128)S(1)} fusion(f32[16384,32]{0,1:T(8,128)} %bitcast.152, bf16[8,33,16384]{2,1,0:T(8,128)(2,1)} %get-tuple-element.261), kind=kLoop, calls=%fused_computation.69 | loop fusion | flops 12451840 | bytes 11010048 | tf_op jit(solution)/shard_map/vz,dvz->dz/dot_general | solution.py:52
  92.2 31.6 %all-gather.8.cloned.1.call-done = f32[16,1,16384]{2,1,0:T(1,128)} async-done(((f32[1,1,16384]{2,1,0:T(1,128)}), f32[16,1,16384]{2,1,0:T(1,128)}) %all-gather.8.cloned.1.call-update) | async-done | bytes 1048592 | tf_op jit(solution)/shard_map/all_gather | solution.py:11
  123.8 1.8 copy.33
  125.6 37.8 %all-gather.10.cloned.1.call-done = f32[16,1,16384]{2,1,0:T(1,128)} async-done(((f32[1,1,16384]{2,1,0:T(1,128)}), f32[16,1,16384]{2,1,0:T(1,128)}) %all-gather.10.cloned.1.call-update) | async-done | bytes 1048592 | tf_op jit(solution)/shard_map/all_gather | solution.py:11
  163.4 2.8 copy.32
  166.2 19.4 %while.44 = (s32[]{:T(128)}, f32[16384]{0:T(1024)S(1)}, f32[16384]{0:T(1024)S(1)}, s32[]{:T(128)}, f32[16,16384]{1,0:T(8,128)S(1)}, /*index=5*/f32[16,16384]{1,0:T(8,128)}, s32[]{:T(128)}, s32[]{:T(128)}) while((s32[]{:T(128)}, f32[16384]{0:T(1024)S(1)}, f32[16384]{0:T(1024)S(1)}, s32[]{:T(128)}, f32[16,16384]{1,0:T(8,128)S(1)}, ...), condition=%wide.region_5.6_spmd.clone, body=%wide.region_4.5_spmd.clone.sunk | while | flops 114692 | bytes 655477 | solution.py:21
  186.3 85.3 %all-reduce.4.cloned.1.call-done = f32[16384]{0:T(1024)} async-done(((f32[16384]{0:T(1024)}), f32[16384]{0:T(1024)}) %all-reduce.4.cloned.1.call-update) | async-done | bytes 65552 | tf_op jit(solution)/shard_map/psum | solution.py:137
  272.8 5.4 %multiply_reduce_fusion = f32[16384,32]{0,1:T(8,128)S(1)} fusion(f32[16384,8]{0,1:T(8,128)S(1)} %get-tuple-element.370, bf16[8,33,16384]{2,1,0:T(8,128)(2,1)} %get-tuple-element.261), kind=kLoop, calls=%fused_computation.68 | loop fusion | flops 12058624 | bytes 11010048 | tf_op jit(solution)/shard_map/vi,vsi->si/dot_general | solution.py:51
  280.2 4.6 multiply_convert_fusion.2
  284.8 9.0 %pad_maximum_fusion.3 = bf16[8,33,16384]{2,1,0:T(8,128)(2,1)} fusion(bf16[8,1,16384]{2,1,0:T(2,128)(2,1)S(1)} %copy.13, bf16[8,32,16384]{2,1,0:T(8,128)(2,1)} %multiply_convert_fusion.2), kind=kLoop, calls=%fused_computation.71 | loop fusion | flops 17301504 | bytes 17301504 | tf_op jit(solution)/shard_map/concatenate | solution.py:78
  293.8 147.4 %while.45 = (s32[]{:T(128)}, f32[64,32]{0,1:T(8,128)S(1)}, f32[33,64]{1,0:T(8,128)S(1)}, bf16[8,32,16384]{2,1,0:T(8,128)(2,1)}, bf16[8,33,16384]{2,1,0:T(8,128)(...) while((s32[]{:T(128)}, f32[64,32]{0,1:T(8,128)S(1)}, ...), condition=%wide.region_9.10_spmd.clone, body=%wide.region_8.9_spmd.clone.sunk | while | flops 434413696 | bytes 81249400 | solution.py:157
  293.8 4.7 multiply_convert_fusion.5
  304.2 1.6 copy-done.7
  305.8 2.0 fusion.95
  307.9 2.1 convolution_add_fusion.4
  312.3 4.7 multiply_convert_fusion.5
  322.6 1.6 copy-done.7
  324.2 2.0 fusion.95
  326.3 2.1 convolution_add_fusion.4
  330.7 4.7 multiply_convert_fusion.5
  338.0 1.4 dynamic-slice_bitcast_fusion.2
  341.0 1.6 copy-done.7
  342.7 2.0 fusion.95
  344.8 2.1 convolution_add_fusion.4
  349.1 4.7 multiply_convert_fusion.5
  359.5 1.6 copy-done.7
  361.1 2.0 fusion.95
  363.2 2.1 convolution_add_fusion.4
  367.5 4.7 multiply_convert_fusion.5
  377.9 1.6 copy-done.7
  379.5 2.0 fusion.95
  381.6 2.1 convolution_add_fusion.4
  386.0 4.7 multiply_convert_fusion.5
  396.3 1.6 copy-done.7
  397.9 2.0 fusion.95
  400.0 2.1 convolution_add_fusion.4
  404.4 4.7 multiply_convert_fusion.5
  414.7 1.6 copy-done.7
  416.3 2.0 fusion.95
  418.4 2.1 convolution_add_fusion.4
  422.8 4.7 multiply_convert_fusion.5
  433.1 1.6 copy-done.7
  434.7 2.0 fusion.95
  436.8 2.1 convolution_add_fusion.4
  441.2 60.3 %all-reduce.1 = (f32[64,32]{0,1:T(8,128)}, f32[33,64]{1,0:T(8,128)}) all-reduce(f32[64,32]{0,1:T(8,128)S(1)} %get-tuple-element.265, f32[33,64]{1,0:T(8,128)S(1)} %get-tuple-element.266), channel_id=1, replica_groups=mesh['groups'=2,'depth'=16] {'depth'}, use_global_device_ids=true, to_apply=%region_10.11 | all-reduce | flops 4160 | bytes 33280 | tf_op jit(solution)/shard_map/psum | solution.py:158
  501.4 1.5 convert_element_type.53
  (226 shorter events, 97.0 us)
Async XLA Ops:
  7.2 76.1 %all-gather.6.cloned.1.call-start = ((), (), s32[]{:S(2)}) async-start(), calls=%async_computation.1 | async-start | bytes 2228224 | tf_op jit(solution)/shard_map/all_gather | solution.py:125
  7.9 115.9 %all-gather.8.cloned.1.call-start = ((), (), s32[]{:S(2)}) async-start(), calls=%async_computation.4 | async-start | bytes 1114112 | tf_op jit(solution)/shard_map/all_gather | solution.py:11
  83.0 80.4 %all-gather.10.cloned.1.call-start = ((), (), s32[]{:S(2)}) async-start(), calls=%async_computation.5 | async-start | bytes 1114112 | tf_op jit(solution)/shard_map/all_gather | solution.py:11
  92.1 179.5 %all-reduce.4.cloned.1.call-start = ((), (), s32[]{:S(2)}) async-start(), calls=%async_computation.3 | async-start | bytes 131072 | tf_op jit(solution)/shard_map/psum | solution.py:137
  186.2 315.2 %reduce-scatter.2.cloned.1.call-start = ((), (), s32[]{:S(2)}) async-start(), calls=%async_computation.2 | async-start | bytes 1114112 | tf_op jit(solution)/shard_map/reduce_scatter | solution.py:131
  278.2 2.0 copy-start.4
  284.8 9.1 %copy-start.5 = (bf16[33,64]{1,0:T(8,128)(2,1)S(1)}, bf16[33,64]{1,0:T(8,128)(2,1)}, u32[]{:S(2)}) copy-start(bf16[33,64]{1,0:T(8,128)(2,1)} %get-tuple-element.627) | copy-start | bytes 12676
  284.8 9.1 %copy-start.6 = (bf16[64,32]{0,1:T(8,128)(2,1)S(1)}, bf16[64,32]{0,1:T(8,128)(2,1)}, u32[]{:S(2)}) copy-start(bf16[64,32]{0,1:T(8,128)(2,1)} %get-tuple-element.628) | copy-start | bytes 12292
  298.6 1.3 copy-start
  303.6 2.2 copy-start.7
  305.8 2.1 copy-start.2
  307.9 2.1 copy-start.3
  307.9 2.2 copy-start.1
  317.0 1.3 copy-start
  322.0 2.2 copy-start.7
  324.2 2.1 copy-start.2
  326.3 2.1 copy-start.3
  326.3 2.2 copy-start.1
  335.4 1.3 copy-start
  340.5 2.2 copy-start.7
  342.7 2.1 copy-start.2
  344.7 2.1 copy-start.3
  344.7 2.2 copy-start.1
  353.8 1.3 copy-start
  358.9 2.2 copy-start.7
  361.1 2.1 copy-start.2
  363.1 2.1 copy-start.3
  363.2 2.2 copy-start.1
  372.3 1.3 copy-start
  377.3 2.2 copy-start.7
  379.5 2.1 copy-start.2
  381.6 2.1 copy-start.3
  381.6 2.2 copy-start.1
  390.7 1.3 copy-start
  395.7 2.2 copy-start.7
  397.9 2.1 copy-start.2
  400.0 2.1 copy-start.3
  400.0 2.2 copy-start.1
  409.1 1.3 copy-start
  414.1 2.2 copy-start.7
  416.3 2.1 copy-start.2
  418.4 2.1 copy-start.3
  418.4 2.2 copy-start.1
  427.5 1.3 copy-start
  432.5 2.2 copy-start.7
  434.7 2.1 copy-start.2
  436.8 2.1 copy-start.3
  436.8 2.2 copy-start.1
Sparse Core Ops, SparseCore 0:
  10.2 44.1 all-gather.5
  83.1 40.6 all-gather.7
  126.5 36.8 all-gather.9
  186.3 85.2 all-reduce.3
  279.5 59.1 reduce-scatter.1
where the time goes:
time: 512 us; the launch traced here: 509 us
  waiting for transfers between devices  155 us (30%)
  matrix products  116 us (23%)
  local copies, waits for them, and re-layouts  79.1 us (15%)
  other arithmetic  72.1 us (14%)
  blocking collectives  60.3 us (12%)
  between operations  13.9 us (3%)
  loops' own time  12 us (2%)
    psum x1, waiting for transfers between devices, shards(): ray_total = lax.psum(enter * running[-1], 'depth')  85.3 us
    all_gather x2, waiting for transfers between devices, carried_in(): everything = jax.tree.map(lambda part: lax.all_gather(part, axis), x)  69.3 us
    psum x1, blocking collectives, shards(): grad_first, grad_second = lax.psum((grads[0], grads[1]), 'depth')  60.3 us
    dot_general x8, matrix products, decode_plane(): preact = jnp.dot(w_first, plane, preferred_element_type=jnp.float32)  37.7 us
    dot_general x16, matrix products, decode_plane(): jnp.dot(decoder_second_weight, hidden, preferred_element_type=jnp.float32)  28.6 us
    while x80, local copies, waits for them, and re-layouts  20.5 us
    dynamic_slice x16, local copies, waits for them, and re-layouts, step(): new = combine(before, jax.tree.map(lambda part: part[k], everything))  18.2 us
    dynamic_update_slice x8, other arithmetic, shards(): slabs = lax.map(forward_plane, (voxels, my_offsets))  18.2 us
  transfers between devices with their start and end apart: 5, of which 3 were waited for; matrix products, arithmetic and copies ran while one was open for 42% of the time, Pallas kernels for 0%

commit v1 on v0

--- a/solution.py
+++ b/solution.py
@@ -4,6 +4,11 @@
 from jax.sharding import PartitionSpec as P
 
 TILE = 128
+
+
+def feed_the_terms(local_array):
+    z1 = lax.all_gather(local_array, "depth")
+    return jnp.sum(z1, 0)
 
 
 def carried_in(x, axis, combine, identity):
@@ -134,7 +139,7 @@
         scatter_dimension=1,
         tiled=True,
     ).astype(jnp.float32)
-    ray_total = lax.psum(enter * running[-1], "depth")
+    ray_total = feed_the_terms(enter * running[-1])
     grad_sheared = slab_gradient(
         passing,
         before,

time: 512 us -> 466 us (0.910)
  waiting for transfers between devices: 155 us -> 107 us
    psum x1 -> x0, waiting for transfers between devices: 85.3 us -> none  [shards(): ray_total = lax.psum(enter * running[-1], 'depth')]
    all_gather x0 -> x1, waiting for transfers between devices: none -> 36.9 us  [feed_the_terms(): z1 = lax.all_gather(local_array, 'depth')]
  transfers between devices with their start and end apart: 5 -> 5, of which waited for: 3 -> 3; matrix products, arithmetic and copies ran while one was open for 42% -> 46% of each run, Pallas kernels for 0% -> 0%
where the time goes in v1:
time: 466 us; the launch traced here: 463 us
  matrix products  116 us (25%)
  waiting for transfers between devices  107 us (23%)
  local copies, waits for them, and re-layouts  80.7 us (17%)
  other arithmetic  73.1 us (16%)
  blocking collectives  60 us (13%)
  between operations  13.9 us (3%)
  loops' own time  12 us (3%)
    all_gather x2, waiting for transfers between devices, carried_in(): everything = jax.tree.map(lambda part: lax.all_gather(part, axis), x)  69.3 us
    psum x1, blocking collectives, shards(): grad_first, grad_second = lax.psum((grads[0], grads[1]), 'depth')  60 us
    dot_general x8, matrix products, decode_plane(): preact = jnp.dot(w_first, plane, preferred_element_type=jnp.float32)  37.7 us
    all_gather x1, waiting for transfers between devices, feed_the_terms(): z1 = lax.all_gather(local_array, 'depth')  36.9 us
    dot_general x16, matrix products, decode_plane(): jnp.dot(decoder_second_weight, hidden, preferred_element_type=jnp.float32)  28.5 us
    while x80, local copies, waits for them, and re-layouts  20.7 us
    dynamic_update_slice x8, other arithmetic, shards(): slabs = lax.map(forward_plane, (voxels, my_offsets))  18.2 us
    dynamic_slice x16, local copies, waits for them, and re-layouts, step(): new = combine(before, jax.tree.map(lambda part: part[k], everything))  18.2 us
  transfers between devices with their start and end apart: 5, of which 3 were waited for; matrix products, arithmetic and copies ran while one was open for 46% of the time, Pallas kernels for 0%

profile of v1, /device:TPU:0, one launch (start us, length us, event | category | flops | bytes accessed | tf_op | source)
XLA Modules:
  0.0 463.4 jit_solution(6832075475053844744)
XLA Ops:
  8.7 59.9 %while.43 = (s32[]{:T(128)}, bf16[8,33,16384]{2,1,0:T(8,128)(2,1)}, bf16[8,32,16384]{2,1,0:T(8,128)(2,1)}, bf16[64,32]{0,1:T(8,128)(2,1)}, bf16[33,64]{1,0:T(8,1...) while((s32[]{:T(128)}, bf16[8,33,16384]{2,1,0:T(8,128)(2,1)}, ...), condition=%wide.region_1.2_spmd, body=%wide.region_0.1_spmd.sunk | while | flops 148111360 | bytes 8865971 | solution.py:129
  9.9 3.1 convolution_bitcast_fusion.7
  13.9 2.3 fusion.82
  17.4 3.1 convolution_bitcast_fusion.7
  21.4 2.3 fusion.82
  24.9 3.1 convolution_bitcast_fusion.7
  28.9 2.3 fusion.82
  32.4 3.1 convolution_bitcast_fusion.7
  36.3 2.3 fusion.82
  39.8 3.1 convolution_bitcast_fusion.7
  43.8 2.3 fusion.82
  47.3 3.1 convolution_bitcast_fusion.7
  51.3 2.3 fusion.82
  54.8 3.1 convolution_bitcast_fusion.7
  58.8 2.3 fusion.82
  62.4 3.1 convolution_bitcast_fusion.7
  66.3 2.3 fusion.82
  68.6 12.2 %copy.14 = bf16[8,33,16384]{2,0,1:T(8,128)(2,1)} copy(bf16[8,33,16384]{2,1,0:T(8,128)(2,1)} %get-tuple-element.261) | data formatting | bytes 17301504 | tf_op jit(solution)/shard_map/while | solution.py:129
  83.3 6.6 %multiply_reduce_fusion.1 = f32[16384,8]{0,1:T(8,128)S(1)} fusion(f32[16384,32]{0,1:T(8,128)} %bitcast.152, bf16[8,33,16384]{2,1,0:T(8,128)(2,1)} %get-tuple-element.261), kind=kLoop, calls=%fused_computation.69 | loop fusion | flops 12451840 | bytes 11010048 | tf_op jit(solution)/shard_map/vz,dvz->dz/dot_general | solution.py:57
  92.2 31.5 %all-gather.12.cloned.1.call-done = f32[16,1,16384]{2,1,0:T(1,128)} async-done(((f32[1,1,16384]{2,1,0:T(1,128)}), f32[16,1,16384]{2,1,0:T(1,128)}) %all-gather.12.cloned.1.call-update) | async-done | bytes 1048592 | tf_op jit(solution)/shard_map/all_gather | solution.py:16
  123.8 1.8 copy.35
  125.6 37.8 %all-gather.14.cloned.1.call-done = f32[16,1,16384]{2,1,0:T(1,128)} async-done(((f32[1,1,16384]{2,1,0:T(1,128)}), f32[16,1,16384]{2,1,0:T(1,128)}) %all-gather.14.cloned.1.call-update) | async-done | bytes 1048592 | tf_op jit(solution)/shard_map/all_gather | solution.py:16
  163.4 2.8 copy.34
  166.2 19.4 %while.44 = (s32[]{:T(128)}, f32[16384]{0:T(1024)S(1)}, f32[16384]{0:T(1024)S(1)}, s32[]{:T(128)}, f32[16,16384]{1,0:T(8,128)S(1)}, /*index=5*/f32[16,16384]{1,0:T(8,128)}, s32[]{:T(128)}, s32[]{:T(128)}) while((s32[]{:T(128)}, f32[16384]{0:T(1024)S(1)}, f32[16384]{0:T(1024)S(1)}, s32[]{:T(128)}, f32[16,16384]{1,0:T(8,128)S(1)}, ...), condition=%wide.region_5.6_spmd.clone, body=%wide.region_4.5_spmd.clone.sunk | while | flops 114692 | bytes 655477 | solution.py:26
  186.3 36.9 %all-gather.10.cloned.1.call-done = f32[262144]{0:T(1024)} async-done(((f32[16384]{0:T(1024)}), f32[262144]{0:T(1024)}) %all-gather.10.cloned.1.call-update) | async-done | bytes 1048592 | tf_op jit(solution)/shard_map/all_gather | solution.py:10
  224.8 2.0 broadcast_multiply_fusion
  226.7 5.4 %multiply_reduce_fusion = f32[16384,32]{0,1:T(8,128)S(1)} fusion(f32[16384,8]{0,1:T(8,128)S(1)} %get-tuple-element.370, bf16[8,33,16384]{2,1,0:T(8,128)(2,1)} %get-tuple-element.261), kind=kLoop, calls=%fused_computation.68 | loop fusion | flops 12058624 | bytes 11010048 | tf_op jit(solution)/shard_map/vi,vsi->si/dot_general | solution.py:56
  234.2 4.6 multiply_convert_fusion.2
  238.8 9.1 %pad_maximum_fusion.3 = bf16[8,33,16384]{2,1,0:T(8,128)(2,1)} fusion(bf16[8,1,16384]{2,1,0:T(2,128)(2,1)S(1)} %copy.15, bf16[8,32,16384]{2,1,0:T(8,128)(2,1)} %multiply_convert_fusion.2), kind=kLoop, calls=%fused_computation.71 | loop fusion | flops 17301504 | bytes 17301504 | tf_op jit(solution)/shard_map/concatenate | solution.py:83
  247.9 147.4 %while.45 = (s32[]{:T(128)}, f32[64,32]{0,1:T(8,128)S(1)}, f32[33,64]{1,0:T(8,128)S(1)}, bf16[8,32,16384]{2,1,0:T(8,128)(2,1)}, bf16[8,33,16384]{2,1,0:T(8,128)(...) while((s32[]{:T(128)}, f32[64,32]{0,1:T(8,128)S(1)}, ...), condition=%wide.region_9.10_spmd.clone, body=%wide.region_8.9_spmd.clone.sunk | while | flops 434413696 | bytes 81249400 | solution.py:162
  247.9 4.7 %multiply_convert_fusion.5 = (bf16[64,16384]{1,0:T(8,128)(2,1)S(1)}, f32[64,16384]{1,0:T(8,128)}) fusion(bf16[64,32]{0,1:T(8,128)(2,1)S(1)} %get-tuple-element.603, bf16[8,32,16384]{2,1,0:T(8,128)(2,1)} %get-tuple-element.602, s32[]{:T(128)S(6)} %copy.57), kind=kOutput, calls=%fused_computation.37.clone.1 | convolution fusion | flops 72351744 | bytes 7344132 | tf_op jit(solution)/shard_map/while/body/eval_jaxpr/dot_general | solution.py:30
  258.2 1.7 copy-done.8
  260.0 2.0 fusion.95
  262.1 2.1 convolution_add_fusion.4
  266.4 4.7 %multiply_convert_fusion.5 = (bf16[64,16384]{1,0:T(8,128)(2,1)S(1)}, f32[64,16384]{1,0:T(8,128)}) fusion(bf16[64,32]{0,1:T(8,128)(2,1)S(1)} %get-tuple-element.603, bf16[8,32,16384]{2,1,0:T(8,128)(2,1)} %get-tuple-element.602, s32[]{:T(128)S(6)} %copy.57), kind=kOutput, calls=%fused_computation.37.clone.1 | convolution fusion | flops 72351744 | bytes 7344132 | tf_op jit(solution)/shard_map/while/body/eval_jaxpr/dot_general | solution.py:30
  276.7 1.7 copy-done.8
  278.4 2.0 fusion.95
  280.5 2.1 convolution_add_fusion.4
  284.9 4.7 %multiply_convert_fusion.5 = (bf16[64,16384]{1,0:T(8,128)(2,1)S(1)}, f32[64,16384]{1,0:T(8,128)}) fusion(bf16[64,32]{0,1:T(8,128)(2,1)S(1)} %get-tuple-element.603, bf16[8,32,16384]{2,1,0:T(8,128)(2,1)} %get-tuple-element.602, s32[]{:T(128)S(6)} %copy.57), kind=kOutput, calls=%fused_computation.37.clone.1 | convolution fusion | flops 72351744 | bytes 7344132 | tf_op jit(solution)/shard_map/while/body/eval_jaxpr/dot_general | solution.py:30
  295.2 1.6 copy-done.8
  296.8 2.0 fusion.95
  298.9 2.1 convolution_add_fusion.4
  303.3 4.7 %multiply_convert_fusion.5 = (bf16[64,16384]{1,0:T(8,128)(2,1)S(1)}, f32[64,16384]{1,0:T(8,128)}) fusion(bf16[64,32]{0,1:T(8,128)(2,1)S(1)} %get-tuple-element.603, bf16[8,32,16384]{2,1,0:T(8,128)(2,1)} %get-tuple-element.602, s32[]{:T(128)S(6)} %copy.57), kind=kOutput, calls=%fused_computation.37.clone.1 | convolution fusion | flops 72351744 | bytes 7344132 | tf_op jit(solution)/shard_map/while/body/eval_jaxpr/dot_general | solution.py:30
  313.6 1.6 copy-done.8
  315.2 2.0 fusion.95
  317.3 2.1 convolution_add_fusion.4
  321.7 4.7 %multiply_convert_fusion.5 = (bf16[64,16384]{1,0:T(8,128)(2,1)S(1)}, f32[64,16384]{1,0:T(8,128)}) fusion(bf16[64,32]{0,1:T(8,128)(2,1)S(1)} %get-tuple-element.603, bf16[8,32,16384]{2,1,0:T(8,128)(2,1)} %get-tuple-element.602, s32[]{:T(128)S(6)} %copy.57), kind=kOutput, calls=%fused_computation.37.clone.1 | convolution fusion | flops 72351744 | bytes 7344132 | tf_op jit(solution)/shard_map/while/body/eval_jaxpr/dot_general | solution.py:30
  332.0 1.6 copy-done.8
  333.6 2.0 fusion.95
  335.7 2.1 convolution_add_fusion.4
  340.1 4.7 %multiply_convert_fusion.5 = (bf16[64,16384]{1,0:T(8,128)(2,1)S(1)}, f32[64,16384]{1,0:T(8,128)}) fusion(bf16[64,32]{0,1:T(8,128)(2,1)S(1)} %get-tuple-element.603, bf16[8,32,16384]{2,1,0:T(8,128)(2,1)} %get-tuple-element.602, s32[]{:T(128)S(6)} %copy.57), kind=kOutput, calls=%fused_computation.37.clone.1 | convolution fusion | flops 72351744 | bytes 7344132 | tf_op jit(solution)/shard_map/while/body/eval_jaxpr/dot_general | solution.py:30
  350.4 1.6 copy-done.8
  352.0 2.0 fusion.95
  354.1 2.1 convolution_add_fusion.4
  358.5 4.7 %multiply_convert_fusion.5 = (bf16[64,16384]{1,0:T(8,128)(2,1)S(1)}, f32[64,16384]{1,0:T(8,128)}) fusion(bf16[64,32]{0,1:T(8,128)(2,1)S(1)} %get-tuple-element.603, bf16[8,32,16384]{2,1,0:T(8,128)(2,1)} %get-tuple-element.602, s32[]{:T(128)S(6)} %copy.57), kind=kOutput, calls=%fused_computation.37.clone.1 | convolution fusion | flops 72351744 | bytes 7344132 | tf_op jit(solution)/shard_map/while/body/eval_jaxpr/dot_general | solution.py:30
  368.8 1.6 copy-done.8
  370.4 2.0 fusion.95
  372.5 2.1 convolution_add_fusion.4
  376.9 4.7 %multiply_convert_fusion.5 = (bf16[64,16384]{1,0:T(8,128)(2,1)S(1)}, f32[64,16384]{1,0:T(8,128)}) fusion(bf16[64,32]{0,1:T(8,128)(2,1)S(1)} %get-tuple-element.603, bf16[8,32,16384]{2,1,0:T(8,128)(2,1)} %get-tuple-element.602, s32[]{:T(128)S(6)} %copy.57), kind=kOutput, calls=%fused_computation.37.clone.1 | convolution fusion | flops 72351744 | bytes 7344132 | tf_op jit(solution)/shard_map/while/body/eval_jaxpr/dot_general | solution.py:30
  387.2 1.6 copy-done.8
  388.8 2.0 fusion.95
  390.9 2.1 convolution_add_fusion.4
  395.3 60.0 %all-reduce.1 = (f32[64,32]{0,1:T(8,128)}, f32[33,64]{1,0:T(8,128)}) all-reduce(f32[64,32]{0,1:T(8,128)S(1)} %get-tuple-element.265, f32[33,64]{1,0:T(8,128)S(1)} %get-tuple-element.266), channel_id=1, replica_groups=mesh['groups'=2,'depth'=16] {'depth'}, use_global_device_ids=true, to_apply=%region_10.11 | all-reduce | flops 4160 | bytes 33280 | tf_op jit(solution)/shard_map/psum | solution.py:163
  455.3 1.5 convert_element_type.53
  (230 shorter events, 98.8 us)
Async XLA Ops:
  7.2 76.1 %all-gather.8.cloned.1.call-start = ((), (), s32[]{:S(2)}) async-start(), calls=%async_computation.1 | async-start | bytes 2228224 | tf_op jit(solution)/shard_map/all_gather | solution.py:130
  7.9 115.9 %all-gather.12.cloned.1.call-start = ((), (), s32[]{:S(2)}) async-start(), calls=%async_computation.4 | async-start | bytes 1114112 | tf_op jit(solution)/shard_map/all_gather | solution.py:16
  83.0 80.4 %all-gather.14.cloned.1.call-start = ((), (), s32[]{:S(2)}) async-start(), calls=%async_computation.5 | async-start | bytes 1114112 | tf_op jit(solution)/shard_map/all_gather | solution.py:16
  92.2 131.0 %all-gather.10.cloned.1.call-start = ((), (), s32[]{:S(2)}) async-start(), calls=%async_computation.3 | async-start | bytes 1114112 | tf_op jit(solution)/shard_map/all_gather | solution.py:10
  186.2 269.1 %reduce-scatter.2.cloned.1.call-start = ((), (), s32[]{:S(2)}) async-start(), calls=%async_computation.2 | async-start | bytes 1114112 | tf_op jit(solution)/shard_map/reduce_scatter | solution.py:136
  232.1 1.2 copy-start.5
  232.1 2.1 copy-start.4
  238.8 9.1 %copy-start.6 = (bf16[33,64]{1,0:T(8,128)(2,1)S(1)}, bf16[33,64]{1,0:T(8,128)(2,1)}, u32[]{:S(2)}) copy-start(bf16[33,64]{1,0:T(8,128)(2,1)} %get-tuple-element.628) | copy-start | bytes 12676
  238.8 9.1 %copy-start.7 = (bf16[64,32]{0,1:T(8,128)(2,1)S(1)}, bf16[64,32]{0,1:T(8,128)(2,1)}, u32[]{:S(2)}) copy-start(bf16[64,32]{0,1:T(8,128)(2,1)} %get-tuple-element.629) | copy-start | bytes 12292
  252.6 1.3 copy-start
  257.7 2.3 copy-start.8
  260.0 2.1 copy-start.2
  262.0 2.1 copy-start.3
  262.0 2.2 copy-start.1
  271.1 1.3 copy-start
  276.2 2.2 copy-start.8
  278.4 2.1 copy-start.2
  280.5 2.1 copy-start.3
  280.5 2.2 copy-start.1
  289.6 1.3 copy-start
  294.6 2.2 copy-start.8
  296.8 2.1 copy-start.2
  298.9 2.1 copy-start.3
  298.9 2.2 copy-start.1
  308.0 1.3 copy-start
  313.0 2.2 copy-start.8
  315.2 2.1 copy-start.2
  317.3 2.1 copy-start.3
  317.3 2.2 copy-start.1
  326.4 1.3 copy-start
  331.4 2.2 copy-start.8
  333.6 2.1 copy-start.2
  335.7 2.1 copy-start.3
  335.7 2.2 copy-start.1
  344.8 1.3 copy-start
  349.8 2.2 copy-start.8
  352.0 2.1 copy-start.2
  354.1 2.1 copy-start.3
  354.1 2.2 copy-start.1
  363.2 1.3 copy-start
  368.2 2.2 copy-start.8
  370.4 2.1 copy-start.2
  372.5 2.1 copy-start.3
  372.5 2.2 copy-start.1
  381.6 1.3 copy-start
  386.6 2.2 copy-start.8
  388.8 2.1 copy-start.2
  390.9 2.1 copy-start.3
  390.9 2.2 copy-start.1
Sparse Core Ops, SparseCore 0:
  10.2 44.1 all-gather.7
  83.1 40.5 all-gather.11
  126.5 36.8 all-gather.13
  186.3 36.8 all-gather.9
  233.4 56.5 reduce-scatter.1
